TPU v7x, 32 devices: a whole 2x2x4 slice. The times are simulated.
32 devices in a mesh: src: 8 (over y, x, core), tgt: 4 (over z).
Axes of the slice: x: 2, y: 2, z: 4, core: 2. Of those that a mesh axis runs over, the one named last changes fastest.
Arguments:
- src_emb: bfloat16 [64, 131072], P(None, 'src'), may hold values from -3 to 3
- tgt_emb: bfloat16 [64, 65536], P(None, 'tgt'), may hold values from -3 to 3
- src_hidden: bfloat16 [64, 131072], P(None, 'src'), may hold values from -4 to 4
- growth: float32 [131072], P('src'), may hold values from -1 to 1
- tgt_mass: float32 [65536], P('tgt'), may hold values from 0.5 to 2
- pair_code: int32 [8, 4, 512], P('src', 'tgt'), may hold values from 0 to 16383, as said below
- pair_count: int32 [8, 4], P('src', 'tgt'), may hold values from 128 to 512, as said below
- block_batch: int32 [1024], P('src'), may hold values from 0 to 31
Outputs:
- src_potential: float32 [131072], P('src')
- tgt_potential: float32 [65536], P('tgt')
- tgt_grad: float32 [64, 65536], P(None, 'tgt')
- adapter_grad: float32 [32, 64, 64], P(('src', 'tgt'))
Inputs may be any that keep to these rules, and one draw needn't show every extreme that they name: `pair_code`: the codes of one device are distinct; among the first 128 entries of each device's list every one of its 128 source blocks and every one of its 128 target blocks appears. `pair_count`: in every draw some device has all 512 entries live.
All inputs are finite; a program needn't handle non-finite values.
Results may differ from a plain program's by a relative error of at most 0.0003.
Values sent between devices are 32-bit elements; how exact they have to be, the bound alone decides.
A program may use at most 192 MiB of HBM per device.

v0:
```python
import math
import jax
import jax.numpy as jnp
from jax import lax
from jax.sharding import PartitionSpec as P

BLK = 128
ENC_DEV = 1
ITERS = 2
entropy_scale = 0.5
update_power = 0.4
highest = lax.Precision.HIGHEST


def rescale(scaling, masses, totals):
    return jnp.sqrt(scaling) * jnp.power(masses / totals, update_power)


def pick_blocks(selector, blocks):
    picked = jnp.einsum(
        "gb,dbi->dgi", selector.astype(jnp.bfloat16), blocks, preferred_element_type=jnp.float32
    )
    return picked.astype(jnp.bfloat16)


def per_device(src_emb, tgt_emb, src_hidden, growth, tgt_mass, pair_code, pair_count, block_batch):
    feat_width = src_emb.shape[0]
    src_blocks = src_emb.shape[1] // BLK
    tgt_blocks = tgt_emb.shape[1] // BLK
    src_cells = src_blocks * BLK
    tgt_cells = tgt_blocks * BLK
    slot_count = pair_code.shape[2]
    group_size = math.gcd(slot_count, 64)
    group_count = slot_count // group_size
    pair_slots = pair_code.reshape(slot_count)
    alive_mask = (jnp.arange(slot_count, dtype=jnp.int32) < pair_count.reshape(())).astype(
        jnp.float32
    )
    src_ids = pair_slots // tgt_blocks
    tgt_ids = pair_slots % tgt_blocks
    src_select = (src_ids[:, None] == jnp.arange(src_blocks, dtype=jnp.int32)[None, :]).astype(
        jnp.float32
    )
    tgt_select = (tgt_ids[:, None] == jnp.arange(tgt_blocks, dtype=jnp.int32)[None, :]).astype(
        jnp.float32
    )
    x_blocks = src_emb.reshape(feat_width, src_blocks, BLK)
    y_blocks = tgt_emb.reshape(feat_width, tgt_blocks, BLK)
    x_norms = jnp.sum(jnp.square(x_blocks.astype(jnp.float32)), axis=0)
    y_norms = jnp.sum(jnp.square(y_blocks.astype(jnp.float32)), axis=0)
    src_sel_groups = src_select.reshape(group_count, group_size, src_blocks)
    tgt_sel_groups = tgt_select.reshape(group_count, group_size, tgt_blocks)

    def kernel_group(inputs):
        src_sel, tgt_sel, alive_group = inputs
        x_part = pick_blocks(src_sel, x_blocks)
        y_part = pick_blocks(tgt_sel, y_blocks)
        inner_prods = jnp.einsum("dgi,dgj->gij", x_part, y_part, preferred_element_type=jnp.float32)
        x_sq = jnp.dot(src_sel, x_norms, precision=highest)
        y_sq = jnp.dot(tgt_sel, y_norms, precision=highest)
        distance = (x_sq[:, :, None] + y_sq[:, None, :] - 2.0 * inner_prods) / feat_width
        return jnp.exp(-distance / entropy_scale) * alive_group[:, None, None]

    kernel = lax.map(
        kernel_group, (src_sel_groups, tgt_sel_groups, alive_mask.reshape(group_count, group_size))
    )
    kernel = kernel.reshape(slot_count, BLK, BLK)
    src_mass = jnp.exp(growth)
    src_scale = jnp.ones((src_cells,), jnp.float32)
    tgt_scale = jnp.ones((tgt_cells,), jnp.float32)
    for iteration in range(ITERS):
        tgt_picked = jnp.dot(tgt_select, tgt_scale.reshape(tgt_blocks, BLK), precision=highest)
        src_picked = jnp.dot(src_select, src_scale.reshape(src_blocks, BLK), precision=highest)
        row_slots = jnp.einsum("pij,pj->pi", kernel, tgt_picked, precision=highest)
        col_slots = jnp.einsum("pij,pi->pj", kernel, src_picked, precision=highest)
        row_part = jnp.dot(src_select.T, row_slots, precision=highest).reshape(src_cells)
        col_part = jnp.dot(tgt_select.T, col_slots, precision=highest).reshape(tgt_cells)
        row_sums = lax.psum(row_part, "tgt")
        col_sums = lax.psum(col_part, "src")
        src_scale, tgt_scale = (
            rescale(src_scale, src_mass, row_sums),
            rescale(tgt_scale, tgt_mass, col_sums),
        )
    src_potential = entropy_scale * jnp.log(src_scale)
    tgt_potential = entropy_scale * jnp.log(tgt_scale)
    src_blocked = src_scale.reshape(src_blocks, BLK)
    tgt_blocked = tgt_scale.reshape(tgt_blocks, BLK)

    def gradient_group(carry, inputs):
        dx_total, dy_total = carry
        src_sel, tgt_sel, kernel_part = inputs
        row_scale = jnp.dot(src_sel, src_blocked, precision=highest)
        col_scale = jnp.dot(tgt_sel, tgt_blocked, precision=highest)
        transport = row_scale[:, :, None] * kernel_part * col_scale[:, None, :]
        plan_bf16 = transport.astype(jnp.bfloat16)
        x_part = pick_blocks(src_sel, x_blocks)
        y_part = pick_blocks(tgt_sel, y_blocks)
        pulled = jnp.einsum("gij,dgj->dgi", plan_bf16, y_part, preferred_element_type=jnp.float32)
        pushed = jnp.einsum("gij,dgi->dgj", plan_bf16, x_part, preferred_element_type=jnp.float32)
        dx_term = jnp.sum(transport, axis=2)[None] * x_part.astype(jnp.float32) - pulled
        dy_term = jnp.sum(transport, axis=1)[None] * y_part.astype(jnp.float32) - pushed
        dx_total = dx_total + jnp.einsum("gb,dgi->dbi", src_sel, dx_term, precision=highest)
        dy_total = dy_total + jnp.einsum("gb,dgi->dbi", tgt_sel, dy_term, precision=highest)
        return ((dx_total, dy_total), None)

    start_grads = (
        jnp.zeros((feat_width, src_blocks, BLK), jnp.float32),
        jnp.zeros((feat_width, tgt_blocks, BLK), jnp.float32),
    )
    (dx_total, dy_total), _ = lax.scan(
        gradient_group,
        start_grads,
        (src_sel_groups, tgt_sel_groups, kernel.reshape(group_count, group_size, BLK, BLK)),
    )
    tgt_grad = lax.psum(dy_total.reshape(feat_width, tgt_cells), "src")
    hidden_blocks = src_hidden.reshape(feat_width, src_blocks, BLK)
    grad_share = lax.psum_scatter(dx_total, "tgt", scatter_dimension=1, tiled=True)
    share_blocks = grad_share.shape[1]
    first_block = lax.axis_index("tgt") * share_blocks
    hidden_share = lax.dynamic_slice_in_dim(hidden_blocks, first_block, share_blocks, 1)
    batch_share = lax.dynamic_slice_in_dim(block_batch, first_block, share_blocks, 0)
    outer = (
        jnp.einsum("dbi,ebi->bde", hidden_share.astype(jnp.float32), grad_share, precision=highest)
        / BLK
    )
    wanted = jnp.arange(ENC_DEV * lax.axis_size(("src", "tgt")), dtype=jnp.int32)
    owners = (batch_share[None, :] == wanted[:, None]).astype(jnp.float32)
    adapter_grad = lax.psum_scatter(
        jnp.einsum("kb,bde->kde", owners, outer, precision=highest),
        ("src", "tgt"),
        scatter_dimension=0,
        tiled=True,
    )
    return (src_potential, tgt_potential, tgt_grad, adapter_grad)


def solution(mesh):
    in_specs = (
        P(None, "src"),
        P(None, "tgt"),
        P(None, "src"),
        P("src"),
        P("tgt"),
        P("src", "tgt", None),
        P("src", "tgt"),
        P("src"),
    )
    out_specs = (P("src"), P("tgt"), P(None, "tgt"), P(("src", "tgt"), None, None))
    return jax.shard_map(
        per_device, mesh=mesh, in_specs=in_specs, out_specs=out_specs, check_vma=False
    )
```

profile of v0, /device:TPU:0, one launch (start us, length us, event | category | flops | bytes accessed | tf_op | source)
XLA Modules:
  0.0 1027.3 jit_solution(16935787503366914984)
XLA Ops:
  17.6 84.6 %while.23 = (s32[]{:T(128)}, f32[8,64,128,128]{3,2,1,0:T(8,128)}, f32[8,64,128]{2,1,0:T(8,128)S(1)}, f32[128,128]{1,0:T(8,128)S(1)}, f32[8,64,128]{2,1,0:T(8,128...) while((s32[]{:T(128)}, f32[8,64,128,128]{3,2,1,0:T(8,128)}, ...), condition=%wide.region_3.4_spmd, body=%wide.region_2.3_spmd.sunk | while | flops 435159040 | bytes 21334412 | solution.py:64
  21.5 6.6 bitcast_dynamic-update-slice_fusion.2
  32.1 6.6 bitcast_dynamic-update-slice_fusion.2
  42.7 6.6 bitcast_dynamic-update-slice_fusion.2
  53.3 6.6 bitcast_dynamic-update-slice_fusion.2
  63.8 6.6 bitcast_dynamic-update-slice_fusion.2
  74.4 6.6 bitcast_dynamic-update-slice_fusion.2
  85.0 6.6 bitcast_dynamic-update-slice_fusion.2
  95.5 6.6 bitcast_dynamic-update-slice_fusion.2
  102.5 55.7 %fusion.97 = f32[512,1,128]{2,1,0:T(1,128)S(1)} fusion(f32[512,128,128]{2,1,0:T(8,128)} %bitcast.228, f32[512,128,1]{1,2,0:T(1,128)S(1)} %bitcast.246), kind=kOutput, calls=%fused_computation.137 | convolution fusion | flops 100663296 | bytes 34078720 | tf_op jit(solution)/shard_map/pij,pj->pi/dot_general | solution.py:74
  160.0 32.0 %fusion.98 = f32[512,1,128]{2,1,0:T(1,128)S(1)} fusion(f32[512,128,128]{2,1,0:T(8,128)} %bitcast.229, f32[512,128,1]{1,2,0:T(1,128)S(1)} %bitcast.248), kind=kOutput, calls=%fused_computation.138 | convolution fusion | flops 100663296 | bytes 34078720 | tf_op jit(solution)/shard_map/pij,pi->pj/dot_general | solution.py:75
  193.1 3.4 all-reduce.6.cloned.1.call-done
  197.7 32.3 %fusion.100 = f32[512,1,128]{2,1,0:T(1,128)S(1)} fusion(f32[512,128,128]{2,1,0:T(8,128)} %bitcast.230, f32[512,128,1]{1,2,0:T(1,128)S(1)} %bitcast.249), kind=kOutput, calls=%fused_computation.140 | convolution fusion | flops 100663296 | bytes 34078720 | tf_op jit(solution)/shard_map/pij,pi->pj/dot_general | solution.py:75
  231.3 53.3 %all-reduce.12.cloned.1.call-done = (f32[16384]{0:T(1024)}, f32[16384]{0:T(1024)}) async-done(((f32[16384]{0:T(1024)}, f32[16384]{0:T(1024)}), (f32[16384]{0:T(1024)}, f32[16384]{0:T(1024)})) %all-reduce.12.cloned.1.call-update) | async-done | bytes 131088 | tf_op jit(solution)/shard_map/psum | solution.py:79
  285.8 55.9 %fusion.99 = f32[512,1,128]{2,1,0:T(1,128)S(1)} fusion(f32[512,128,128]{2,1,0:T(8,128)} %bitcast.231, f32[512,128,1]{1,2,0:T(1,128)S(1)} %bitcast.247), kind=kOutput, calls=%fused_computation.139 | convolution fusion | flops 100663296 | bytes 34078720 | tf_op jit(solution)/shard_map/pij,pj->pi/dot_general | solution.py:74
  343.7 33.0 %all-reduce.8.cloned.1.call-done = f32[16384]{0:T(1024)} async-done(((f32[16384]{0:T(1024)}), f32[16384]{0:T(1024)}) %all-reduce.8.cloned.1.call-update) | async-done | bytes 65552 | tf_op jit(solution)/shard_map/psum | solution.py:78
  378.3 330.9 %while.24 = (s32[]{:T(128)}, f32[64,128,128]{1,2,0:T(8,128)}, f32[64,128,128]{1,2,0:T(8,128)}, f32[8,64,128]{2,1,0:T(8,128)S(1)}, f32[128,128]{1,0:T(8,128)}, /*...) while((s32[]{:T(128)}, f32[64,128,128]{1,2,0:T(8,128)}, ...), condition=%wide.region_11.12_spmd.clone, body=%wide.region_8.11_spmd.clone.sunk | while | flops 2191507456 | bytes 61508292 | solution.py:110
  381.0 5.4 fusion.193
  386.5 4.2 fusion.192
  392.9 10.6 %bitcast_add_fusion.5 = f32[64,128,128]{1,2,0:T(8,128)} fusion(f32[64,128,128]{1,2,0:T(8,128)} %get-tuple-element.360, f32[64,64,128]{2,1,0:T(8,128)} %fusion.193, bf16[64,64,128]{2,1,0:T(8,128)(2,1)} %fusion.187, pred[]{:T(512)S(6)} %compare.16, f32[64,128]{1,0:T(8,128)S(1)} %get-tuple-element.315, f32[8,64,128]{2,1,0:T(8,128)} %get-tuple-element.376, ...), kind=kOutput, calls=%fused_computation.23.clone.1 | convolution fusion | flops 808976384 | bytes 11600385 | tf_op jit(solution)/shard_map/while/body/eval_jaxpr/gb,dgi->dbi/dot_general | solution.py:103
  403.5 4.7 fusion.190
  408.2 9.7 bitcast_add_fusion.4
  420.5 5.4 fusion.193
  425.9 4.2 fusion.192
  432.3 11.2 %bitcast_add_fusion.5 = f32[64,128,128]{1,2,0:T(8,128)} fusion(f32[64,128,128]{1,2,0:T(8,128)} %get-tuple-element.360, f32[64,64,128]{2,1,0:T(8,128)} %fusion.193, bf16[64,64,128]{2,1,0:T(8,128)(2,1)} %fusion.187, pred[]{:T(512)S(6)} %compare.16, f32[64,128]{1,0:T(8,128)S(1)} %get-tuple-element.315, f32[8,64,128]{2,1,0:T(8,128)} %get-tuple-element.376, ...), kind=kOutput, calls=%fused_computation.23.clone.1 | convolution fusion | flops 808976384 | bytes 11600385 | tf_op jit(solution)/shard_map/while/body/eval_jaxpr/gb,dgi->dbi/dot_general | solution.py:103
  443.5 4.7 fusion.190
  448.2 11.3 %bitcast_add_fusion.4 = f32[64,128,128]{1,2,0:T(8,128)} fusion(f32[64,128,128]{1,2,0:T(8,128)} %get-tuple-element.359, f32[64,64,128]{2,1,0:T(8,128)S(1)} %fusion.190, bf16[64,64,128]{2,1,0:T(8,128)(2,1)S(1)} %fusion.191, pred[]{:T(512)S(6)} %compare.16, f32[64,128]{1,0:T(8,128)S(1)} %get-tuple-element.314, ...), kind=kOutput, calls=%fused_computation.24.clone.1 | convolution fusion | flops 808976384 | bytes 11599877 | tf_op jit(solution)/shard_map/while/body/eval_jaxpr/gb,dgi->dbi/dot_general | solution.py:102
  462.0 5.4 fusion.193
  467.5 4.2 fusion.192
  473.9 11.2 %bitcast_add_fusion.5 = f32[64,128,128]{1,2,0:T(8,128)} fusion(f32[64,128,128]{1,2,0:T(8,128)} %get-tuple-element.360, f32[64,64,128]{2,1,0:T(8,128)} %fusion.193, bf16[64,64,128]{2,1,0:T(8,128)(2,1)} %fusion.187, pred[]{:T(512)S(6)} %compare.16, f32[64,128]{1,0:T(8,128)S(1)} %get-tuple-element.315, f32[8,64,128]{2,1,0:T(8,128)} %get-tuple-element.376, ...), kind=kOutput, calls=%fused_computation.23.clone.1 | convolution fusion | flops 808976384 | bytes 11600385 | tf_op jit(solution)/shard_map/while/body/eval_jaxpr/gb,dgi->dbi/dot_general | solution.py:103
  485.1 4.7 fusion.190
  489.8 11.3 %bitcast_add_fusion.4 = f32[64,128,128]{1,2,0:T(8,128)} fusion(f32[64,128,128]{1,2,0:T(8,128)} %get-tuple-element.359, f32[64,64,128]{2,1,0:T(8,128)S(1)} %fusion.190, bf16[64,64,128]{2,1,0:T(8,128)(2,1)S(1)} %fusion.191, pred[]{:T(512)S(6)} %compare.16, f32[64,128]{1,0:T(8,128)S(1)} %get-tuple-element.314, ...), kind=kOutput, calls=%fused_computation.24.clone.1 | convolution fusion | flops 808976384 | bytes 11599877 | tf_op jit(solution)/shard_map/while/body/eval_jaxpr/gb,dgi->dbi/dot_general | solution.py:102
  503.6 5.4 fusion.193
  509.0 4.2 fusion.192
  515.5 11.2 %bitcast_add_fusion.5 = f32[64,128,128]{1,2,0:T(8,128)} fusion(f32[64,128,128]{1,2,0:T(8,128)} %get-tuple-element.360, f32[64,64,128]{2,1,0:T(8,128)} %fusion.193, bf16[64,64,128]{2,1,0:T(8,128)(2,1)} %fusion.187, pred[]{:T(512)S(6)} %compare.16, f32[64,128]{1,0:T(8,128)S(1)} %get-tuple-element.315, f32[8,64,128]{2,1,0:T(8,128)} %get-tuple-element.376, ...), kind=kOutput, calls=%fused_computation.23.clone.1 | convolution fusion | flops 808976384 | bytes 11600385 | tf_op jit(solution)/shard_map/while/body/eval_jaxpr/gb,dgi->dbi/dot_general | solution.py:103
  526.7 4.7 fusion.190
  531.4 11.3 %bitcast_add_fusion.4 = f32[64,128,128]{1,2,0:T(8,128)} fusion(f32[64,128,128]{1,2,0:T(8,128)} %get-tuple-element.359, f32[64,64,128]{2,1,0:T(8,128)S(1)} %fusion.190, bf16[64,64,128]{2,1,0:T(8,128)(2,1)S(1)} %fusion.191, pred[]{:T(512)S(6)} %compare.16, f32[64,128]{1,0:T(8,128)S(1)} %get-tuple-element.314, ...), kind=kOutput, calls=%fused_computation.24.clone.1 | convolution fusion | flops 808976384 | bytes 11599877 | tf_op jit(solution)/shard_map/while/body/eval_jaxpr/gb,dgi->dbi/dot_general | solution.py:102
  545.2 5.4 fusion.193
  550.6 4.2 fusion.192
  557.0 11.2 %bitcast_add_fusion.5 = f32[64,128,128]{1,2,0:T(8,128)} fusion(f32[64,128,128]{1,2,0:T(8,128)} %get-tuple-element.360, f32[64,64,128]{2,1,0:T(8,128)} %fusion.193, bf16[64,64,128]{2,1,0:T(8,128)(2,1)} %fusion.187, pred[]{:T(512)S(6)} %compare.16, f32[64,128]{1,0:T(8,128)S(1)} %get-tuple-element.315, f32[8,64,128]{2,1,0:T(8,128)} %get-tuple-element.376, ...), kind=kOutput, calls=%fused_computation.23.clone.1 | convolution fusion | flops 808976384 | bytes 11600385 | tf_op jit(solution)/shard_map/while/body/eval_jaxpr/gb,dgi->dbi/dot_general | solution.py:103
  568.2 4.7 fusion.190
  572.9 11.3 %bitcast_add_fusion.4 = f32[64,128,128]{1,2,0:T(8,128)} fusion(f32[64,128,128]{1,2,0:T(8,128)} %get-tuple-element.359, f32[64,64,128]{2,1,0:T(8,128)S(1)} %fusion.190, bf16[64,64,128]{2,1,0:T(8,128)(2,1)S(1)} %fusion.191, pred[]{:T(512)S(6)} %compare.16, f32[64,128]{1,0:T(8,128)S(1)} %get-tuple-element.314, ...), kind=kOutput, calls=%fused_computation.24.clone.1 | convolution fusion | flops 808976384 | bytes 11599877 | tf_op jit(solution)/shard_map/while/body/eval_jaxpr/gb,dgi->dbi/dot_general | solution.py:102
  586.7 5.4 fusion.193
  592.2 4.2 fusion.192
  598.6 11.2 %bitcast_add_fusion.5 = f32[64,128,128]{1,2,0:T(8,128)} fusion(f32[64,128,128]{1,2,0:T(8,128)} %get-tuple-element.360, f32[64,64,128]{2,1,0:T(8,128)} %fusion.193, bf16[64,64,128]{2,1,0:T(8,128)(2,1)} %fusion.187, pred[]{:T(512)S(6)} %compare.16, f32[64,128]{1,0:T(8,128)S(1)} %get-tuple-element.315, f32[8,64,128]{2,1,0:T(8,128)} %get-tuple-element.376, ...), kind=kOutput, calls=%fused_computation.23.clone.1 | convolution fusion | flops 808976384 | bytes 11600385 | tf_op jit(solution)/shard_map/while/body/eval_jaxpr/gb,dgi->dbi/dot_general | solution.py:103
  609.8 4.7 fusion.190
  614.5 11.3 %bitcast_add_fusion.4 = f32[64,128,128]{1,2,0:T(8,128)} fusion(f32[64,128,128]{1,2,0:T(8,128)} %get-tuple-element.359, f32[64,64,128]{2,1,0:T(8,128)S(1)} %fusion.190, bf16[64,64,128]{2,1,0:T(8,128)(2,1)S(1)} %fusion.191, pred[]{:T(512)S(6)} %compare.16, f32[64,128]{1,0:T(8,128)S(1)} %get-tuple-element.314, ...), kind=kOutput, calls=%fused_computation.24.clone.1 | convolution fusion | flops 808976384 | bytes 11599877 | tf_op jit(solution)/shard_map/while/body/eval_jaxpr/gb,dgi->dbi/dot_general | solution.py:102
  628.3 5.4 fusion.193
  633.7 4.2 fusion.192
  640.2 11.2 %bitcast_add_fusion.5 = f32[64,128,128]{1,2,0:T(8,128)} fusion(f32[64,128,128]{1,2,0:T(8,128)} %get-tuple-element.360, f32[64,64,128]{2,1,0:T(8,128)} %fusion.193, bf16[64,64,128]{2,1,0:T(8,128)(2,1)} %fusion.187, pred[]{:T(512)S(6)} %compare.16, f32[64,128]{1,0:T(8,128)S(1)} %get-tuple-element.315, f32[8,64,128]{2,1,0:T(8,128)} %get-tuple-element.376, ...), kind=kOutput, calls=%fused_computation.23.clone.1 | convolution fusion | flops 808976384 | bytes 11600385 | tf_op jit(solution)/shard_map/while/body/eval_jaxpr/gb,dgi->dbi/dot_general | solution.py:103
  651.4 4.7 fusion.190
  656.1 11.3 %bitcast_add_fusion.4 = f32[64,128,128]{1,2,0:T(8,128)} fusion(f32[64,128,128]{1,2,0:T(8,128)} %get-tuple-element.359, f32[64,64,128]{2,1,0:T(8,128)S(1)} %fusion.190, bf16[64,64,128]{2,1,0:T(8,128)(2,1)S(1)} %fusion.191, pred[]{:T(512)S(6)} %compare.16, f32[64,128]{1,0:T(8,128)S(1)} %get-tuple-element.314, ...), kind=kOutput, calls=%fused_computation.24.clone.1 | convolution fusion | flops 808976384 | bytes 11599877 | tf_op jit(solution)/shard_map/while/body/eval_jaxpr/gb,dgi->dbi/dot_general | solution.py:102
  669.9 5.4 fusion.193
  675.3 4.2 fusion.192
  681.7 11.2 %bitcast_add_fusion.5 = f32[64,128,128]{1,2,0:T(8,128)} fusion(f32[64,128,128]{1,2,0:T(8,128)} %get-tuple-element.360, f32[64,64,128]{2,1,0:T(8,128)} %fusion.193, bf16[64,64,128]{2,1,0:T(8,128)(2,1)} %fusion.187, pred[]{:T(512)S(6)} %compare.16, f32[64,128]{1,0:T(8,128)S(1)} %get-tuple-element.315, f32[8,64,128]{2,1,0:T(8,128)} %get-tuple-element.376, ...), kind=kOutput, calls=%fused_computation.23.clone.1 | convolution fusion | flops 808976384 | bytes 11600385 | tf_op jit(solution)/shard_map/while/body/eval_jaxpr/gb,dgi->dbi/dot_general | solution.py:103
  693.0 4.7 fusion.190
  697.7 11.3 %bitcast_add_fusion.4 = f32[64,128,128]{1,2,0:T(8,128)} fusion(f32[64,128,128]{1,2,0:T(8,128)} %get-tuple-element.359, f32[64,64,128]{2,1,0:T(8,128)S(1)} %fusion.190, bf16[64,64,128]{2,1,0:T(8,128)(2,1)S(1)} %fusion.191, pred[]{:T(512)S(6)} %compare.16, f32[64,128]{1,0:T(8,128)S(1)} %get-tuple-element.314, ...), kind=kOutput, calls=%fused_computation.24.clone.1 | convolution fusion | flops 808976384 | bytes 11599877 | tf_op jit(solution)/shard_map/while/body/eval_jaxpr/gb,dgi->dbi/dot_general | solution.py:102
  709.1 5.4 copy.15
  714.6 5.6 copy.14
  720.2 6.9 copy.62
  729.5 61.7 %reduce-scatter.3.cloned.1.call-done = f32[64,32,128]{2,0,1:T(8,128)} async-done(((f32[64,128,128]{2,0,1:T(8,128)}), f32[64,32,128]{2,0,1:T(8,128)}) %reduce-scatter.3.cloned.1.call-update) | async-done | bytes 1048592 | tf_op jit(solution)/shard_map/reduce_scatter | solution.py:117
  796.3 79.4 %all-reduce.10.cloned.1.call-done = f32[64,16384]{1,0:T(8,128)} async-done(((f32[64,16384]{1,0:T(8,128)}), f32[64,16384]{1,0:T(8,128)}) %all-reduce.10.cloned.1.call-update) | async-done | bytes 4194320 | tf_op jit(solution)/shard_map/psum | solution.py:115
  875.7 139.8 %reduce-scatter.5.cloned.1.call-done = f32[1,64,64]{2,1,0:T(8,128)} async-done(((f32[32,64,64]{2,1,0:T(8,128)}), f32[1,64,64]{2,1,0:T(8,128)}) %reduce-scatter.5.cloned.1.call-update) | async-done | bytes 16400 | tf_op jit(solution)/shard_map/reduce_scatter | solution.py:128
  1015.5 4.5 copy.97
  (178 shorter events, 96.2 us)
Async XLA Ops:
  7.2 189.4 %all-reduce.6.cloned.1.call-start = ((), (), s32[]{:S(2)}) async-start(), calls=%async_computation.2 | async-start | bytes 131072 | tf_op jit(solution)/shard_map/psum | solution.py:78
  9.2 4.4 copy-start.3
  17.6 84.6 %copy-start.9 = (s32[1,1,512]{2,1,0:T(1,128)S(1)}, s32[1,1,512]{2,1,0:T(1,128)}, u32[]{:S(2)}) copy-start(s32[1,1,512]{2,1,0:T(1,128)} %param.17) | copy-start | bytes 6148
  17.6 1.6 copy-start
  28.1 1.6 copy-start
  38.7 1.6 copy-start
  49.3 1.6 copy-start
  59.9 1.6 copy-start
  70.4 1.6 copy-start
  81.0 1.6 copy-start
  91.6 1.6 copy-start
  159.4 125.2 %all-reduce.12.cloned.1.call-start = ((), (), s32[]{:S(2)}) async-start(), calls=%async_computation.7 | async-start | bytes 262144 | tf_op jit(solution)/shard_map/psum | solution.py:79
  160.0 36.6 %copy-start.5 = (f32[16384]{0:T(1024)S(1)}, f32[16384]{0:T(1024)}, u32[]{:S(2)}) copy-start(f32[16384]{0:T(1024)} %param.15) | copy-start | bytes 196612
  197.7 86.9 %copy-start.4 = (f32[16384]{0:T(1024)S(1)}, f32[16384]{0:T(1024)}, u32[]{:S(2)}) copy-start(f32[16384]{0:T(1024)} %param.16) | copy-start | bytes 196612
  231.2 145.4 %all-reduce.8.cloned.1.call-start = ((), (), s32[]{:S(2)}) async-start(), calls=%async_computation.3 | async-start | bytes 131072 | tf_op jit(solution)/shard_map/psum | solution.py:78
  285.8 57.1 %copy-start.7 = (f32[16384]{0:T(1024)S(1)}, f32[16384]{0:T(1024)}, u32[]{:S(2)}) copy-start(f32[16384]{0:T(1024)} %get-tuple-element.184) | copy-start | bytes 196612
  285.8 57.1 %copy-start.8 = (f32[16384]{0:T(1024)S(1)}, f32[16384]{0:T(1024)}, u32[]{:S(2)}) copy-start(f32[16384]{0:T(1024)} %get-tuple-element.185) | copy-start | bytes 196612
  285.8 90.9 %copy-start.6 = (f32[16384]{0:T(1024)S(1)}, f32[16384]{0:T(1024)}, u32[]{:S(2)}) copy-start(f32[16384]{0:T(1024)} %all-reduce.6.cloned.1.call-done) | copy-start | bytes 196612
  342.8 448.4 %reduce-scatter.3.cloned.1.call-start = ((), (), s32[]{:S(2)}) async-start(), calls=%async_computation.5 | async-start | bytes 5242880 | tf_op jit(solution)/shard_map/reduce_scatter | solution.py:117
  381.0 9.7 copy-start.1
  392.9 10.6 %copy-start.2 = (bf16[64,64,128]{2,1,0:T(8,128)(2,1)S(1)}, bf16[64,64,128]{2,1,0:T(8,128)(2,1)}, u32[]{:S(2)}) copy-start(bf16[64,64,128]{2,1,0:T(8,128)(2,1)} %fusion.187) | copy-start | bytes 3145732 | tf_op jit(solution)/shard_map/while
  420.4 9.7 copy-start.1
  432.3 11.2 %copy-start.2 = (bf16[64,64,128]{2,1,0:T(8,128)(2,1)S(1)}, bf16[64,64,128]{2,1,0:T(8,128)(2,1)}, u32[]{:S(2)}) copy-start(bf16[64,64,128]{2,1,0:T(8,128)(2,1)} %fusion.187) | copy-start | bytes 3145732 | tf_op jit(solution)/shard_map/while
  462.0 9.7 copy-start.1
  473.9 11.2 %copy-start.2 = (bf16[64,64,128]{2,1,0:T(8,128)(2,1)S(1)}, bf16[64,64,128]{2,1,0:T(8,128)(2,1)}, u32[]{:S(2)}) copy-start(bf16[64,64,128]{2,1,0:T(8,128)(2,1)} %fusion.187) | copy-start | bytes 3145732 | tf_op jit(solution)/shard_map/while
  503.6 9.7 copy-start.1
  515.5 11.2 %copy-start.2 = (bf16[64,64,128]{2,1,0:T(8,128)(2,1)S(1)}, bf16[64,64,128]{2,1,0:T(8,128)(2,1)}, u32[]{:S(2)}) copy-start(bf16[64,64,128]{2,1,0:T(8,128)(2,1)} %fusion.187) | copy-start | bytes 3145732 | tf_op jit(solution)/shard_map/while
  545.2 9.7 copy-start.1
  557.0 11.2 %copy-start.2 = (bf16[64,64,128]{2,1,0:T(8,128)(2,1)S(1)}, bf16[64,64,128]{2,1,0:T(8,128)(2,1)}, u32[]{:S(2)}) copy-start(bf16[64,64,128]{2,1,0:T(8,128)(2,1)} %fusion.187) | copy-start | bytes 3145732 | tf_op jit(solution)/shard_map/while
  586.7 9.7 copy-start.1
  598.6 11.2 %copy-start.2 = (bf16[64,64,128]{2,1,0:T(8,128)(2,1)S(1)}, bf16[64,64,128]{2,1,0:T(8,128)(2,1)}, u32[]{:S(2)}) copy-start(bf16[64,64,128]{2,1,0:T(8,128)(2,1)} %fusion.187) | copy-start | bytes 3145732 | tf_op jit(solution)/shard_map/while
  628.3 9.7 copy-start.1
  640.2 11.2 %copy-start.2 = (bf16[64,64,128]{2,1,0:T(8,128)(2,1)S(1)}, bf16[64,64,128]{2,1,0:T(8,128)(2,1)}, u32[]{:S(2)}) copy-start(bf16[64,64,128]{2,1,0:T(8,128)(2,1)} %fusion.187) | copy-start | bytes 3145732 | tf_op jit(solution)/shard_map/while
  669.9 9.7 copy-start.1
  681.7 11.2 %copy-start.2 = (bf16[64,64,128]{2,1,0:T(8,128)(2,1)S(1)}, bf16[64,64,128]{2,1,0:T(8,128)(2,1)}, u32[]{:S(2)}) copy-start(bf16[64,64,128]{2,1,0:T(8,128)(2,1)} %fusion.187) | copy-start | bytes 3145732 | tf_op jit(solution)/shard_map/while
  714.6 161.1 %all-reduce.10.cloned.1.call-start = ((), (), s32[]{:S(2)}) async-start(), calls=%async_computation.4 | async-start | bytes 8388608 | tf_op jit(solution)/shard_map/psum | solution.py:115
  727.1 2.3 copy-start.10
  727.2 288.3 %reduce-scatter.5.cloned.1.call-start = ((), (), s32[]{:S(2)}) async-start(), calls=%async_computation.6 | async-start | bytes 1081344 | tf_op jit(solution)/shard_map/reduce_scatter | solution.py:128
Sparse Core Ops, SparseCore 0:
  159.5 36.9 all-reduce.5
  231.4 53.2 all-reduce.11
  343.0 33.6 all-reduce.7
  714.7 76.4 reduce-scatter.2
  794.3 81.3 all-reduce.9
  878.4 137.0 reduce-scatter.4
where the time goes:
time: 1040 us; the launch traced here: 1030 us
  matrix products  558 us (54%)
  waiting for transfers between devices  371 us (36%)
  other arithmetic  41.4 us (4%)
  local copies, waits for them, and re-layouts  40.3 us (4%)
  between operations  15.4 us (1%)
    reduce_scatter x1, waiting for transfers between devices, per_device(): lax.psum_scatter(jnp.einsum('kb,bde->kde', owners, outer, precision=highe...  140 us
    dot_general x2, matrix products, per_device(): row_slots = jnp.einsum('pij,pj->pi', kernel, tgt_picked, precision=highest)  112 us
    dot_general x8, matrix products, gradient_group(): jnp.einsum('gb,dgi->dbi', tgt_sel, dy_term, precision=highest)  89 us
    dot_general x8, matrix products, gradient_group(): jnp.einsum('gb,dgi->dbi', src_sel, dx_term, precision=highest)  88.5 us
    psum x1, waiting for transfers between devices, per_device(): tgt_grad = lax.psum(dy_total.reshape(feat_width, tgt_cells), 'src')  79.4 us
    dot_general x2, matrix products, per_device(): col_slots = jnp.einsum('pij,pi->pj', kernel, src_picked, precision=highest)  64.3 us
    reduce_scatter x1, waiting for transfers between devices, per_device(): lax.psum_scatter(dx_total, 'tgt', scatter_dimension=1, tiled=True)  61.7 us
    psum x1, waiting for transfers between devices, per_device(): col_sums = lax.psum(col_part, 'src')  53.3 us
  transfers between devices with their start and end apart: 6, of which 6 were waited for; matrix products, arithmetic and copies ran while one was open for 5% of the time, Pallas kernels for 0%

commit v1 on v0

--- a/solution.py
+++ b/solution.py
@@ -112,7 +112,7 @@
         start_grads,
         (src_sel_groups, tgt_sel_groups, kernel.reshape(group_count, group_size, BLK, BLK)),
     )
-    tgt_grad = lax.psum(dy_total.reshape(feat_width, tgt_cells), "src")
+    tgt_grad = jnp.sum(lax.all_gather(dy_total.reshape(feat_width, tgt_cells), "src"), axis=0)
     hidden_blocks = src_hidden.reshape(feat_width, src_blocks, BLK)
     grad_share = lax.psum_scatter(dx_total, "tgt", scatter_dimension=1, tiled=True)
     share_blocks = grad_share.shape[1]

time: 1040 us -> 1110 us (1.067)
  waiting for transfers between devices: 371 us -> 437 us
  local copies, waits for them, and re-layouts: 40.3 us -> 25 us
  other arithmetic: 41.4 us -> 55.4 us
    all_gather x0 -> x1, waiting for transfers between devices: none -> 158 us  [per_device(): lax.all_gather(dy_total.reshape(feat_width, tgt_cells), 'src')]
    psum x1 -> x0, waiting for transfers between devices: 79.4 us -> none  [per_device(): tgt_grad = lax.psum(dy_total.reshape(feat_width, tgt_cells), 'src')]
    reduce_sum x0 -> x1, other arithmetic: none -> 14 us  [per_device(): jnp.sum(lax.all_gather(dy_total.reshape(feat_width, tgt_cells), 'src'), a...]
    reduce_scatter x1, waiting for transfers between devices: 140 us -> 126 us  [per_device(): lax.psum_scatter(jnp.einsum('kb,bde->kde', owners, outer, precision=highe...]
    unnamed x22 -> x20, local copies, waits for them, and re-layouts: 18.2 us -> 6.76 us
  transfers between devices with their start and end apart: 6 -> 6, of which waited for: 6 -> 6; matrix products, arithmetic and copies ran while one was open for 5% -> 6% of each run, Pallas kernels for 0% -> 0%
where the time goes in v1:
time: 1110 us; the launch traced here: 1100 us
  matrix products  565 us (51%)
  waiting for transfers between devices  437 us (39%)
  other arithmetic  55.4 us (5%)
  local copies, waits for them, and re-layouts  25 us (2%)
  between operations  15.4 us (1%)
    all_gather x1, waiting for transfers between devices, per_device(): lax.all_gather(dy_total.reshape(feat_width, tgt_cells), 'src')  158 us
    reduce_scatter x1, waiting for transfers between devices, per_device(): lax.psum_scatter(jnp.einsum('kb,bde->kde', owners, outer, precision=highe...  126 us
    dot_general x2, matrix products, per_device(): row_slots = jnp.einsum('pij,pj->pi', kernel, tgt_picked, precision=highest)  112 us
    dot_general x8, matrix products, gradient_group(): jnp.einsum('gb,dgi->dbi', tgt_sel, dy_term, precision=highest)  89 us
    dot_general x8, matrix products, gradient_group(): jnp.einsum('gb,dgi->dbi', src_sel, dx_term, precision=highest)  88.5 us
    dot_general x2, matrix products, per_device(): col_slots = jnp.einsum('pij,pi->pj', kernel, src_picked, precision=highest)  64.3 us
    reduce_scatter x1, waiting for transfers between devices, per_device(): lax.psum_scatter(dx_total, 'tgt', scatter_dimension=1, tiled=True)  63.3 us
    psum x1, waiting for transfers between devices, per_device(): col_sums = lax.psum(col_part, 'src')  53.3 us
  transfers between devices with their start and end apart: 6, of which 6 were waited for; matrix products, arithmetic and copies ran while one was open for 6% of the time, Pallas kernels for 0%

profile of v1, /device:TPU:0, one launch (start us, length us, event | category | flops | bytes accessed | tf_op | source)
XLA Modules:
  0.0 1099.0 jit_solution(15945523939458369130)
XLA Ops:
  17.6 82.1 %while.23 = (s32[]{:T(128)}, f32[8,64,128,128]{3,2,1,0:T(8,128)}, f32[8,64,128]{2,1,0:T(8,128)S(1)}, f32[128,128]{1,0:T(8,128)S(1)}, f32[8,64,128]{2,1,0:T(8,128...) while((s32[]{:T(128)}, f32[8,64,128,128]{3,2,1,0:T(8,128)}, ...), condition=%wide.region_3.4_spmd, body=%wide.region_2.3_spmd.sunk | while | flops 436207616 | bytes 12945777 | solution.py:64
  21.2 6.6 bitcast_dynamic-update-slice_fusion.2
  31.5 6.6 bitcast_dynamic-update-slice_fusion.2
  41.8 6.6 bitcast_dynamic-update-slice_fusion.2
  52.0 6.6 bitcast_dynamic-update-slice_fusion.2
  62.3 6.6 bitcast_dynamic-update-slice_fusion.2
  72.5 6.6 bitcast_dynamic-update-slice_fusion.2
  82.8 6.6 bitcast_dynamic-update-slice_fusion.2
  93.1 6.6 bitcast_dynamic-update-slice_fusion.2
  100.0 55.7 %fusion.93 = f32[512,1,128]{2,1,0:T(1,128)S(1)} fusion(f32[512,128,128]{2,1,0:T(8,128)} %bitcast.222, f32[512,128,1]{1,2,0:T(1,128)S(1)} %bitcast.238), kind=kOutput, calls=%fused_computation.134 | convolution fusion | flops 100663296 | bytes 34078720 | tf_op jit(solution)/shard_map/pij,pj->pi/dot_general | solution.py:74
  157.5 32.0 %fusion.94 = f32[512,1,128]{2,1,0:T(1,128)S(1)} fusion(f32[512,128,128]{2,1,0:T(8,128)} %bitcast.223, f32[512,128,1]{1,2,0:T(1,128)S(1)} %bitcast.240), kind=kOutput, calls=%fused_computation.135 | convolution fusion | flops 100663296 | bytes 34078720 | tf_op jit(solution)/shard_map/pij,pi->pj/dot_general | solution.py:75
  190.6 3.5 all-reduce.5.cloned.1.call-done
  195.3 32.3 %fusion.96 = f32[512,1,128]{2,1,0:T(1,128)S(1)} fusion(f32[512,128,128]{2,1,0:T(8,128)} %bitcast.224, f32[512,128,1]{1,2,0:T(1,128)S(1)} %bitcast.241), kind=kOutput, calls=%fused_computation.137 | convolution fusion | flops 100663296 | bytes 34078720 | tf_op jit(solution)/shard_map/pij,pi->pj/dot_general | solution.py:75
  228.8 53.3 %all-reduce.9.cloned.1.call-done = (f32[16384]{0:T(1024)}, f32[16384]{0:T(1024)}) async-done(((f32[16384]{0:T(1024)}, f32[16384]{0:T(1024)}), (f32[16384]{0:T(1024)}, f32[16384]{0:T(1024)})) %all-reduce.9.cloned.1.call-update) | async-done | bytes 131088 | tf_op jit(solution)/shard_map/psum | solution.py:79
  283.3 55.9 %fusion.95 = f32[512,1,128]{2,1,0:T(1,128)S(1)} fusion(f32[512,128,128]{2,1,0:T(8,128)} %bitcast.225, f32[512,128,1]{1,2,0:T(1,128)S(1)} %bitcast.239), kind=kOutput, calls=%fused_computation.136 | convolution fusion | flops 100663296 | bytes 34078720 | tf_op jit(solution)/shard_map/pij,pj->pi/dot_general | solution.py:74
  341.2 33.0 %all-reduce.7.cloned.1.call-done = f32[16384]{0:T(1024)} async-done(((f32[16384]{0:T(1024)}), f32[16384]{0:T(1024)}) %all-reduce.7.cloned.1.call-update) | async-done | bytes 65552 | tf_op jit(solution)/shard_map/psum | solution.py:78
  375.8 330.8 %while.24 = (s32[]{:T(128)}, f32[64,128,128]{1,2,0:T(8,128)}, f32[64,128,128]{1,2,0:T(8,128)}, f32[8,64,128]{2,1,0:T(8,128)S(1)}, f32[128,128]{1,0:T(8,128)}, /*...) while((s32[]{:T(128)}, f32[64,128,128]{1,2,0:T(8,128)}, ...), condition=%wide.region_11.12_spmd.clone, body=%wide.region_8.11_spmd.clone.sunk | while | flops 2191507456 | bytes 61508292 | solution.py:110
  378.6 5.4 fusion.189
  384.0 4.2 fusion.188
  390.4 10.6 bitcast_add_fusion.5
  401.0 4.7 fusion.186
  405.7 9.7 bitcast_add_fusion.4
  418.0 5.4 fusion.189
  423.4 4.2 fusion.188
  429.8 11.2 %bitcast_add_fusion.5 = f32[64,128,128]{1,2,0:T(8,128)} fusion(f32[64,128,128]{1,2,0:T(8,128)} %get-tuple-element.364, f32[64,64,128]{2,1,0:T(8,128)} %fusion.189, bf16[64,64,128]{2,1,0:T(8,128)(2,1)} %fusion.183, pred[]{:T(512)S(6)} %compare.16, f32[64,128]{1,0:T(8,128)S(1)} %get-tuple-element.319, f32[8,64,128]{2,1,0:T(8,128)} %get-tuple-element.380, ...), kind=kOutput, calls=%fused_computation.23.clone.1 | convolution fusion | flops 808976384 | bytes 11600385 | tf_op jit(solution)/shard_map/while/body/eval_jaxpr/gb,dgi->dbi/dot_general | solution.py:103
  441.0 4.7 fusion.186
  445.7 11.3 %bitcast_add_fusion.4 = f32[64,128,128]{1,2,0:T(8,128)} fusion(f32[64,128,128]{1,2,0:T(8,128)} %get-tuple-element.363, f32[64,64,128]{2,1,0:T(8,128)S(1)} %fusion.186, bf16[64,64,128]{2,1,0:T(8,128)(2,1)S(1)} %fusion.187, pred[]{:T(512)S(6)} %compare.16, f32[64,128]{1,0:T(8,128)S(1)} %get-tuple-element.318, ...), kind=kOutput, calls=%fused_computation.24.clone.1 | convolution fusion | flops 808976384 | bytes 11599877 | tf_op jit(solution)/shard_map/while/body/eval_jaxpr/gb,dgi->dbi/dot_general | solution.py:102
  459.5 5.4 fusion.189
  464.9 4.2 fusion.188
  471.4 11.2 %bitcast_add_fusion.5 = f32[64,128,128]{1,2,0:T(8,128)} fusion(f32[64,128,128]{1,2,0:T(8,128)} %get-tuple-element.364, f32[64,64,128]{2,1,0:T(8,128)} %fusion.189, bf16[64,64,128]{2,1,0:T(8,128)(2,1)} %fusion.183, pred[]{:T(512)S(6)} %compare.16, f32[64,128]{1,0:T(8,128)S(1)} %get-tuple-element.319, f32[8,64,128]{2,1,0:T(8,128)} %get-tuple-element.380, ...), kind=kOutput, calls=%fused_computation.23.clone.1 | convolution fusion | flops 808976384 | bytes 11600385 | tf_op jit(solution)/shard_map/while/body/eval_jaxpr/gb,dgi->dbi/dot_general | solution.py:103
  482.6 4.7 fusion.186
  487.3 11.3 %bitcast_add_fusion.4 = f32[64,128,128]{1,2,0:T(8,128)} fusion(f32[64,128,128]{1,2,0:T(8,128)} %get-tuple-element.363, f32[64,64,128]{2,1,0:T(8,128)S(1)} %fusion.186, bf16[64,64,128]{2,1,0:T(8,128)(2,1)S(1)} %fusion.187, pred[]{:T(512)S(6)} %compare.16, f32[64,128]{1,0:T(8,128)S(1)} %get-tuple-element.318, ...), kind=kOutput, calls=%fused_computation.24.clone.1 | convolution fusion | flops 808976384 | bytes 11599877 | tf_op jit(solution)/shard_map/while/body/eval_jaxpr/gb,dgi->dbi/dot_general | solution.py:102
  501.1 5.4 fusion.189
  506.5 4.2 fusion.188
  512.9 11.2 %bitcast_add_fusion.5 = f32[64,128,128]{1,2,0:T(8,128)} fusion(f32[64,128,128]{1,2,0:T(8,128)} %get-tuple-element.364, f32[64,64,128]{2,1,0:T(8,128)} %fusion.189, bf16[64,64,128]{2,1,0:T(8,128)(2,1)} %fusion.183, pred[]{:T(512)S(6)} %compare.16, f32[64,128]{1,0:T(8,128)S(1)} %get-tuple-element.319, f32[8,64,128]{2,1,0:T(8,128)} %get-tuple-element.380, ...), kind=kOutput, calls=%fused_computation.23.clone.1 | convolution fusion | flops 808976384 | bytes 11600385 | tf_op jit(solution)/shard_map/while/body/eval_jaxpr/gb,dgi->dbi/dot_general | solution.py:103
  524.1 4.7 fusion.186
  528.9 11.3 %bitcast_add_fusion.4 = f32[64,128,128]{1,2,0:T(8,128)} fusion(f32[64,128,128]{1,2,0:T(8,128)} %get-tuple-element.363, f32[64,64,128]{2,1,0:T(8,128)S(1)} %fusion.186, bf16[64,64,128]{2,1,0:T(8,128)(2,1)S(1)} %fusion.187, pred[]{:T(512)S(6)} %compare.16, f32[64,128]{1,0:T(8,128)S(1)} %get-tuple-element.318, ...), kind=kOutput, calls=%fused_computation.24.clone.1 | convolution fusion | flops 808976384 | bytes 11599877 | tf_op jit(solution)/shard_map/while/body/eval_jaxpr/gb,dgi->dbi/dot_general | solution.py:102
  542.6 5.4 fusion.189
  548.1 4.2 fusion.188
  554.5 11.2 %bitcast_add_fusion.5 = f32[64,128,128]{1,2,0:T(8,128)} fusion(f32[64,128,128]{1,2,0:T(8,128)} %get-tuple-element.364, f32[64,64,128]{2,1,0:T(8,128)} %fusion.189, bf16[64,64,128]{2,1,0:T(8,128)(2,1)} %fusion.183, pred[]{:T(512)S(6)} %compare.16, f32[64,128]{1,0:T(8,128)S(1)} %get-tuple-element.319, f32[8,64,128]{2,1,0:T(8,128)} %get-tuple-element.380, ...), kind=kOutput, calls=%fused_computation.23.clone.1 | convolution fusion | flops 808976384 | bytes 11600385 | tf_op jit(solution)/shard_map/while/body/eval_jaxpr/gb,dgi->dbi/dot_general | solution.py:103
  565.7 4.7 fusion.186
  570.4 11.3 %bitcast_add_fusion.4 = f32[64,128,128]{1,2,0:T(8,128)} fusion(f32[64,128,128]{1,2,0:T(8,128)} %get-tuple-element.363, f32[64,64,128]{2,1,0:T(8,128)S(1)} %fusion.186, bf16[64,64,128]{2,1,0:T(8,128)(2,1)S(1)} %fusion.187, pred[]{:T(512)S(6)} %compare.16, f32[64,128]{1,0:T(8,128)S(1)} %get-tuple-element.318, ...), kind=kOutput, calls=%fused_computation.24.clone.1 | convolution fusion | flops 808976384 | bytes 11599877 | tf_op jit(solution)/shard_map/while/body/eval_jaxpr/gb,dgi->dbi/dot_general | solution.py:102
  584.2 5.4 fusion.189
  589.6 4.2 fusion.188
  596.1 11.2 %bitcast_add_fusion.5 = f32[64,128,128]{1,2,0:T(8,128)} fusion(f32[64,128,128]{1,2,0:T(8,128)} %get-tuple-element.364, f32[64,64,128]{2,1,0:T(8,128)} %fusion.189, bf16[64,64,128]{2,1,0:T(8,128)(2,1)} %fusion.183, pred[]{:T(512)S(6)} %compare.16, f32[64,128]{1,0:T(8,128)S(1)} %get-tuple-element.319, f32[8,64,128]{2,1,0:T(8,128)} %get-tuple-element.380, ...), kind=kOutput, calls=%fused_computation.23.clone.1 | convolution fusion | flops 808976384 | bytes 11600385 | tf_op jit(solution)/shard_map/while/body/eval_jaxpr/gb,dgi->dbi/dot_general | solution.py:103
  607.3 4.7 fusion.186
  612.0 11.3 %bitcast_add_fusion.4 = f32[64,128,128]{1,2,0:T(8,128)} fusion(f32[64,128,128]{1,2,0:T(8,128)} %get-tuple-element.363, f32[64,64,128]{2,1,0:T(8,128)S(1)} %fusion.186, bf16[64,64,128]{2,1,0:T(8,128)(2,1)S(1)} %fusion.187, pred[]{:T(512)S(6)} %compare.16, f32[64,128]{1,0:T(8,128)S(1)} %get-tuple-element.318, ...), kind=kOutput, calls=%fused_computation.24.clone.1 | convolution fusion | flops 808976384 | bytes 11599877 | tf_op jit(solution)/shard_map/while/body/eval_jaxpr/gb,dgi->dbi/dot_general | solution.py:102
  625.8 5.4 fusion.189
  631.2 4.2 fusion.188
  637.6 11.2 %bitcast_add_fusion.5 = f32[64,128,128]{1,2,0:T(8,128)} fusion(f32[64,128,128]{1,2,0:T(8,128)} %get-tuple-element.364, f32[64,64,128]{2,1,0:T(8,128)} %fusion.189, bf16[64,64,128]{2,1,0:T(8,128)(2,1)} %fusion.183, pred[]{:T(512)S(6)} %compare.16, f32[64,128]{1,0:T(8,128)S(1)} %get-tuple-element.319, f32[8,64,128]{2,1,0:T(8,128)} %get-tuple-element.380, ...), kind=kOutput, calls=%fused_computation.23.clone.1 | convolution fusion | flops 808976384 | bytes 11600385 | tf_op jit(solution)/shard_map/while/body/eval_jaxpr/gb,dgi->dbi/dot_general | solution.py:103
  648.8 4.7 fusion.186
  653.5 11.3 %bitcast_add_fusion.4 = f32[64,128,128]{1,2,0:T(8,128)} fusion(f32[64,128,128]{1,2,0:T(8,128)} %get-tuple-element.363, f32[64,64,128]{2,1,0:T(8,128)S(1)} %fusion.186, bf16[64,64,128]{2,1,0:T(8,128)(2,1)S(1)} %fusion.187, pred[]{:T(512)S(6)} %compare.16, f32[64,128]{1,0:T(8,128)S(1)} %get-tuple-element.318, ...), kind=kOutput, calls=%fused_computation.24.clone.1 | convolution fusion | flops 808976384 | bytes 11599877 | tf_op jit(solution)/shard_map/while/body/eval_jaxpr/gb,dgi->dbi/dot_general | solution.py:102
  667.3 5.4 fusion.189
  672.8 4.2 fusion.188
  679.2 11.2 %bitcast_add_fusion.5 = f32[64,128,128]{1,2,0:T(8,128)} fusion(f32[64,128,128]{1,2,0:T(8,128)} %get-tuple-element.364, f32[64,64,128]{2,1,0:T(8,128)} %fusion.189, bf16[64,64,128]{2,1,0:T(8,128)(2,1)} %fusion.183, pred[]{:T(512)S(6)} %compare.16, f32[64,128]{1,0:T(8,128)S(1)} %get-tuple-element.319, f32[8,64,128]{2,1,0:T(8,128)} %get-tuple-element.380, ...), kind=kOutput, calls=%fused_computation.23.clone.1 | convolution fusion | flops 808976384 | bytes 11600385 | tf_op jit(solution)/shard_map/while/body/eval_jaxpr/gb,dgi->dbi/dot_general | solution.py:103
  690.4 4.7 fusion.186
  695.1 11.3 %bitcast_add_fusion.4 = f32[64,128,128]{1,2,0:T(8,128)} fusion(f32[64,128,128]{1,2,0:T(8,128)} %get-tuple-element.363, f32[64,64,128]{2,1,0:T(8,128)S(1)} %fusion.186, bf16[64,64,128]{2,1,0:T(8,128)(2,1)S(1)} %fusion.187, pred[]{:T(512)S(6)} %compare.16, f32[64,128]{1,0:T(8,128)S(1)} %get-tuple-element.318, ...), kind=kOutput, calls=%fused_computation.24.clone.1 | convolution fusion | flops 808976384 | bytes 11599877 | tf_op jit(solution)/shard_map/while/body/eval_jaxpr/gb,dgi->dbi/dot_general | solution.py:102
  706.6 5.4 copy.33
  712.1 5.6 copy.31
  717.7 5.3 all_gather_reshape.3
  725.3 63.3 %reduce-scatter.3.cloned.1.call-done = f32[64,32,128]{2,0,1:T(8,128)} async-done(((f32[64,128,128]{2,0,1:T(8,128)}), f32[64,32,128]{2,0,1:T(8,128)}) %reduce-scatter.3.cloned.1.call-update) | async-done | bytes 1048592 | tf_op jit(solution)/shard_map/reduce_scatter | solution.py:117
  793.8 157.8 %all-gather.2.cloned.1.call-done = f32[8,64,16384]{2,1,0:T(8,128)} async-done(((f32[1,64,16384]{2,1,0:T(8,128)}), f32[8,64,16384]{2,1,0:T(8,128)}) %all-gather.2.cloned.1.call-update) | async-done | bytes 33554448 | tf_op jit(solution)/shard_map/all_gather | solution.py:115
  951.6 14.0 %reduce_sum.53 = f32[64,16384]{1,0:T(8,128)} reduce(f32[8,64,16384]{2,1,0:T(8,128)} %all-gather.2.cloned.1.call-done, f32[]{:T(128)} %constant.71.clone.1), dimensions={0}, to_apply=%region_12.13 | reduce | flops 7340032 | bytes 37748740 | tf_op jit(solution)/shard_map/reduce_sum | solution.py:115
  965.6 126.1 %reduce-scatter.5.cloned.1.call-done = f32[1,64,64]{2,1,0:T(8,128)} async-done(((f32[32,64,64]{2,1,0:T(8,128)}), f32[1,64,64]{2,1,0:T(8,128)}) %reduce-scatter.5.cloned.1.call-update) | async-done | bytes 16400 | tf_op jit(solution)/shard_map/reduce_scatter | solution.py:128
  (162 shorter events, 93.8 us)
Async XLA Ops:
  7.2 186.9 %all-reduce.5.cloned.1.call-start = ((), (), s32[]{:S(2)}) async-start(), calls=%async_computation.2 | async-start | bytes 131072 | tf_op jit(solution)/shard_map/psum | solution.py:78
  9.2 4.4 copy-start.2
  17.6 82.1 %copy-start.8 = (s32[1,1,512]{2,1,0:T(1,128)S(1)}, s32[1,1,512]{2,1,0:T(1,128)}, u32[]{:S(2)}) copy-start(s32[1,1,512]{2,1,0:T(1,128)} %param.17) | copy-start | bytes 6148
  156.9 125.2 %all-reduce.9.cloned.1.call-start = ((), (), s32[]{:S(2)}) async-start(), calls=%async_computation.7 | async-start | bytes 262144 | tf_op jit(solution)/shard_map/psum | solution.py:79
  157.5 36.6 %copy-start.4 = (f32[16384]{0:T(1024)S(1)}, f32[16384]{0:T(1024)}, u32[]{:S(2)}) copy-start(f32[16384]{0:T(1024)} %param.15) | copy-start | bytes 196612
  195.2 86.9 %copy-start.3 = (f32[16384]{0:T(1024)S(1)}, f32[16384]{0:T(1024)}, u32[]{:S(2)}) copy-start(f32[16384]{0:T(1024)} %param.16) | copy-start | bytes 196612
  228.8 145.4 %all-reduce.7.cloned.1.call-start = ((), (), s32[]{:S(2)}) async-start(), calls=%async_computation.3 | async-start | bytes 131072 | tf_op jit(solution)/shard_map/psum | solution.py:78
  283.3 57.1 %copy-start.6 = (f32[16384]{0:T(1024)S(1)}, f32[16384]{0:T(1024)}, u32[]{:S(2)}) copy-start(f32[16384]{0:T(1024)} %get-tuple-element.188) | copy-start | bytes 196612
  283.3 57.1 %copy-start.7 = (f32[16384]{0:T(1024)S(1)}, f32[16384]{0:T(1024)}, u32[]{:S(2)}) copy-start(f32[16384]{0:T(1024)} %get-tuple-element.189) | copy-start | bytes 196612
  283.3 90.9 %copy-start.5 = (f32[16384]{0:T(1024)S(1)}, f32[16384]{0:T(1024)}, u32[]{:S(2)}) copy-start(f32[16384]{0:T(1024)} %all-reduce.5.cloned.1.call-done) | copy-start | bytes 196612
  340.4 448.3 %reduce-scatter.3.cloned.1.call-start = ((), (), s32[]{:S(2)}) async-start(), calls=%async_computation.5 | async-start | bytes 5242880 | tf_op jit(solution)/shard_map/reduce_scatter | solution.py:117
  378.5 9.7 copy-start
  390.4 10.6 copy-start.1
  417.9 9.7 copy-start
  429.8 11.2 %copy-start.1 = (bf16[64,64,128]{2,1,0:T(8,128)(2,1)S(1)}, bf16[64,64,128]{2,1,0:T(8,128)(2,1)}, u32[]{:S(2)}) copy-start(bf16[64,64,128]{2,1,0:T(8,128)(2,1)} %fusion.183) | copy-start | bytes 3145732 | tf_op jit(solution)/shard_map/while
  459.5 9.7 copy-start
  471.4 11.2 %copy-start.1 = (bf16[64,64,128]{2,1,0:T(8,128)(2,1)S(1)}, bf16[64,64,128]{2,1,0:T(8,128)(2,1)}, u32[]{:S(2)}) copy-start(bf16[64,64,128]{2,1,0:T(8,128)(2,1)} %fusion.183) | copy-start | bytes 3145732 | tf_op jit(solution)/shard_map/while
  501.1 9.7 copy-start
  512.9 11.2 %copy-start.1 = (bf16[64,64,128]{2,1,0:T(8,128)(2,1)S(1)}, bf16[64,64,128]{2,1,0:T(8,128)(2,1)}, u32[]{:S(2)}) copy-start(bf16[64,64,128]{2,1,0:T(8,128)(2,1)} %fusion.183) | copy-start | bytes 3145732 | tf_op jit(solution)/shard_map/while
  542.6 9.7 copy-start
  554.5 11.2 %copy-start.1 = (bf16[64,64,128]{2,1,0:T(8,128)(2,1)S(1)}, bf16[64,64,128]{2,1,0:T(8,128)(2,1)}, u32[]{:S(2)}) copy-start(bf16[64,64,128]{2,1,0:T(8,128)(2,1)} %fusion.183) | copy-start | bytes 3145732 | tf_op jit(solution)/shard_map/while
  584.2 9.7 copy-start
  596.1 11.2 %copy-start.1 = (bf16[64,64,128]{2,1,0:T(8,128)(2,1)S(1)}, bf16[64,64,128]{2,1,0:T(8,128)(2,1)}, u32[]{:S(2)}) copy-start(bf16[64,64,128]{2,1,0:T(8,128)(2,1)} %fusion.183) | copy-start | bytes 3145732 | tf_op jit(solution)/shard_map/while
  625.8 9.7 copy-start
  637.6 11.2 %copy-start.1 = (bf16[64,64,128]{2,1,0:T(8,128)(2,1)S(1)}, bf16[64,64,128]{2,1,0:T(8,128)(2,1)}, u32[]{:S(2)}) copy-start(bf16[64,64,128]{2,1,0:T(8,128)(2,1)} %fusion.183) | copy-start | bytes 3145732 | tf_op jit(solution)/shard_map/while
  667.3 9.7 copy-start
  679.2 11.2 %copy-start.1 = (bf16[64,64,128]{2,1,0:T(8,128)(2,1)S(1)}, bf16[64,64,128]{2,1,0:T(8,128)(2,1)}, u32[]{:S(2)}) copy-start(bf16[64,64,128]{2,1,0:T(8,128)(2,1)} %fusion.183) | copy-start | bytes 3145732 | tf_op jit(solution)/shard_map/while
  712.0 239.6 %all-gather.2.cloned.1.call-start = ((), (), s32[]{:S(2)}) async-start(), calls=%async_computation.4 | async-start | bytes 37748736 | tf_op jit(solution)/shard_map/all_gather | solution.py:115
  723.0 2.3 copy-start.9
  723.0 368.7 %reduce-scatter.5.cloned.1.call-start = ((), (), s32[]{:S(2)}) async-start(), calls=%async_computation.6 | async-start | bytes 1081344 | tf_op jit(solution)/shard_map/reduce_scatter | solution.py:128
Sparse Core Ops, SparseCore 0:
  157.0 37.0 all-reduce.4
  228.9 53.2 all-reduce.8
  340.5 33.6 all-reduce.6
  712.1 76.4 reduce-scatter.2
  790.4 161.1 all-gather.1
  954.3 137.3 reduce-scatter.4
